TPU v7x, 128 devices: a whole 4x4x4 slice. The times are simulated.
128 devices in a mesh: dp: 4 (over x), tensor: 32 (over y, z, core).
Axes of the slice: x: 4, y: 4, z: 4, core: 2. Of those that a mesh axis runs over, the one named last changes fastest.
Arguments:
- tokens: bfloat16 [16384, 2048], P(('dp', 'tensor')), may hold values from -6 to 6
- norm_gain: bfloat16 [2048], replicated, may hold values from 0.099609375 to 1.8984375
- routes: int32 [16384, 6], P(('dp', 'tensor')), may hold values from 0 to 31, all different within a row; in each aligned block of 128 rows (0 to 127, 128 to 255, ...) at most 32 rows name the same one
- route_gates: bfloat16 [16384, 6], P(('dp', 'tensor')), may hold values from 0.19921875 to 1
- lengths: int32 [24], replicated, may hold values from 1 to 1920, 16384 in all
- request_adapter: int32 [24], replicated, may hold values from 0 to 31
- adapter_slot: int32 [32], replicated, may hold values from 0 to 31, each once
- expert_gate: bfloat16 [32, 2048, 1408], P('tensor'), may hold values from -0.125 to 0.125
- expert_up: bfloat16 [32, 2048, 1408], P('tensor'), may hold values from -0.125 to 0.125
- expert_down: bfloat16 [32, 1408, 2048], P('tensor'), may hold values from -0.15625 to 0.15625
- shared_gate: bfloat16 [2048, 1408], P(None, 'dp'), may hold values from -0.125 to 0.125
- shared_up_weight: bfloat16 [2048, 1408], P(None, 'dp'), may hold values from -0.125 to 0.125
- shared_down: bfloat16 [1408, 2048], P('dp'), may hold values from -0.15625 to 0.15625
- adapter_down: bfloat16 [32, 2048, 16], P('dp'), may hold values from -0.125 to 0.125
- adapter_up: bfloat16 [32, 16, 2048], P('dp'), may hold values from -1.5 to 1.5
- head_weight: bfloat16 [2048, 65536], P(None, ('dp', 'tensor')), may hold values from -0.375 to 0.375
Outputs:
- sublayer_out: bfloat16 [16384, 2048], P(('dp', 'tensor'))
- last_norm: float32 [24], replicated
- block_logit: float32 [24, 32], P(None, 'tensor')
Inputs may be any that keep to these rules, and one draw needn't show every extreme that they name: `routes`: in each aligned block of 128 rows (the rows of one device), no expert is named by more than 32 rows, a bound that some block reaches. The lengths sum to 16384; the largest is exactly 1920. Each position of the store appears once: adapter a is stored at position adapter_slot[a] of adapter_down and adapter_up.
All inputs are finite; a program needn't handle non-finite values.
Results may differ from a plain program's by a relative error of at most 0.0066.
Values may be sent and summed in bfloat16 or wider, within the bound.
A program may use at most 128 MiB of HBM per device.

v0:
```python
import jax
import jax.numpy as jnp
from jax import lax
from jax.sharding import PartitionSpec as P

CAP = 32


def apply_norm(tokens, norm_gain):
    values = tokens.astype(jnp.float32)
    scaled = lax.rsqrt(jnp.mean(values * values, axis=-1, keepdims=True) + 1e-06)
    return (values * scaled * norm_gain.astype(jnp.float32)).astype(jnp.bfloat16)


def feed_forward(inputs, gate_mat, up_mat, down_mat):
    gate_portion = jnp.dot(inputs, gate_mat, preferred_element_type=jnp.float32)
    up_part = jnp.dot(inputs, up_mat, preferred_element_type=jnp.float32)
    hidden = (jax.nn.silu(gate_portion) * up_part).astype(jnp.bfloat16)
    return jnp.dot(hidden, down_mat, preferred_element_type=jnp.float32)


def token_slots(positions, lengths, request_adapter, adapter_slot):
    request_ends = jnp.cumsum(lengths)
    request = jnp.sum((request_ends[None, :] <= positions[:, None]).astype(jnp.int32), axis=1)
    request_pick = (
        request[:, None] == jnp.arange(request_adapter.shape[0], dtype=jnp.int32)[None, :]
    )
    adapter = jnp.sum(jnp.where(request_pick, request_adapter[None, :], 0), axis=1)
    adapter_pick = adapter[:, None] == jnp.arange(adapter_slot.shape[0], dtype=jnp.int32)[None, :]
    return jnp.sum(jnp.where(adapter_pick, adapter_slot[None, :], 0), axis=1)


def adapter_delta(inputs, slot_ids, down_store, up_store):
    held_count = down_store.shape[0]
    model_width = down_store.shape[1]
    rank_size = down_store.shape[2]
    flat_down = jnp.transpose(down_store, (1, 0, 2)).reshape(model_width, held_count * rank_size)
    low_rank = jnp.dot(inputs, flat_down, preferred_element_type=jnp.float32)
    low_rank = low_rank.reshape(inputs.shape[0], held_count, rank_size)
    keep_mask = slot_ids[:, None] == jnp.arange(held_count, dtype=jnp.int32)[None, :]
    low_rank = jnp.where(keep_mask[:, :, None], low_rank, 0.0).astype(jnp.bfloat16)
    low_rank = low_rank.reshape(inputs.shape[0], held_count * rank_size)
    flat_up = up_store.reshape(held_count * rank_size, up_store.shape[2])
    return jnp.dot(low_rank, flat_up, preferred_element_type=jnp.float32)


def local(
    tokens,
    norm_gain,
    routes,
    route_gates,
    lengths,
    request_adapter,
    adapter_slot,
    expert_gate,
    expert_up,
    expert_down,
    shared_gate,
    shared_up_weight,
    shared_down,
    adapter_down,
    adapter_up,
    head_weight,
):
    tok_rows = tokens.shape[0]
    model_width = tokens.shape[1]
    route_count = routes.shape[1]
    tensor_size = lax.axis_size("tensor")
    tensor_pos = lax.axis_index("tensor")
    data_pos = lax.axis_index("dp")
    local_experts = expert_gate.shape[0]
    all_experts = local_experts * tensor_size
    slot_range = jnp.arange(CAP, dtype=jnp.int32)
    normed = apply_norm(tokens, norm_gain)
    numbers = jnp.arange(all_experts, dtype=jnp.int32)
    route_hits = routes[:, :, None] == numbers[None, None, :]
    chosen = jnp.any(route_hits, axis=1)
    weight = jnp.sum(
        jnp.where(route_hits, route_gates[:, :, None], jnp.zeros((), jnp.bfloat16)), axis=1
    )
    slot_place = jnp.cumsum(chosen.astype(jnp.int32), axis=0) - 1
    pooled, pooled_routes = (
        lax.all_gather(normed, "tensor", axis=0, tiled=True),
        lax.all_gather(routes.astype(jnp.bfloat16), "tensor", axis=0, tiled=True),
    )
    pooled = pooled.reshape(tensor_size, tok_rows, model_width)
    source_routes = pooled_routes.astype(jnp.int32).reshape(tensor_size, tok_rows, route_count)
    own_numbers = tensor_pos * local_experts + jnp.arange(local_experts, dtype=jnp.int32)
    source_hits = source_routes[:, :, :, None] == own_numbers[None, None, None, :]
    source_chosen = jnp.any(source_hits, axis=2)
    source_place = jnp.cumsum(source_chosen.astype(jnp.int32), axis=1) - 1
    source_pick = source_chosen[:, :, :, None] & (
        source_place[:, :, :, None] == slot_range[None, None, None, :]
    )
    source_pick = jnp.where(source_pick, 1.0, 0.0).astype(jnp.bfloat16)
    incoming = jnp.einsum(
        "sijc,sid->sjcd", source_pick, pooled, preferred_element_type=jnp.float32
    ).astype(jnp.bfloat16)
    gate_portion = jnp.einsum(
        "secd,edf->secf", incoming, expert_gate, preferred_element_type=jnp.float32
    )
    up_part = jnp.einsum("secd,edf->secf", incoming, expert_up, preferred_element_type=jnp.float32)
    hidden = (jax.nn.silu(gate_portion) * up_part).astype(jnp.bfloat16)
    expert_out = jnp.einsum(
        "secf,efd->secd", hidden, expert_down, preferred_element_type=jnp.float32
    ).astype(jnp.bfloat16)
    returned_rows = lax.all_to_all(expert_out, "tensor", split_axis=0, concat_axis=0, tiled=True)
    returned_rows = returned_rows.reshape(all_experts, CAP, model_width)
    mixing_result = jnp.where(
        slot_place[:, :, None] == slot_range[None, None, :],
        weight[:, :, None],
        jnp.zeros((), jnp.bfloat16),
    )
    routed_output = jnp.einsum(
        "kbt,btw->kw", mixing_result, returned_rows, preferred_element_type=jnp.float32
    )
    own_base = (data_pos * tensor_size + tensor_pos) * tok_rows
    own_positions = own_base + jnp.arange(tok_rows, dtype=jnp.int32)
    peer_rows = lax.all_gather(normed, "dp", axis=0, tiled=True)
    shared_sum = lax.psum_scatter(
        feed_forward(peer_rows, shared_gate, shared_up_weight, shared_down),
        "dp",
        scatter_dimension=0,
        tiled=True,
    )
    own_slots = token_slots(own_positions, lengths, request_adapter, adapter_slot)
    store_down, store_up = (
        lax.all_gather(adapter_down, "dp", axis=0, tiled=True),
        lax.all_gather(adapter_up, "dp", axis=0, tiled=True),
    )
    summed = routed_output + shared_sum + adapter_delta(normed, own_slots, store_down, store_up)
    sublayer_out = summed.astype(jnp.bfloat16)
    request_ends = jnp.cumsum(lengths)
    last_pick = jnp.where(request_ends[:, None] - 1 == own_positions[None, :], 1.0, 0.0).astype(
        jnp.bfloat16
    )
    last_part = jnp.dot(last_pick, sublayer_out, preferred_element_type=jnp.float32)
    last_states = lax.psum(last_part, ("dp", "tensor"))
    last_norm = jnp.sqrt(jnp.sum(last_states * last_states, axis=1))
    logits = jnp.dot(
        last_states.astype(jnp.bfloat16), head_weight, preferred_element_type=jnp.float32
    )
    block_logit = lax.pmax(jnp.max(logits, axis=1), "dp")
    return (sublayer_out, last_norm, block_logit[:, None])


def solution(mesh):
    placed = (
        P(("dp", "tensor"), None),
        P(),
        P(("dp", "tensor"), None),
        P(("dp", "tensor"), None),
        P(),
        P(),
        P(),
        P("tensor", None, None),
        P("tensor", None, None),
        P("tensor", None, None),
        P(None, "dp"),
        P(None, "dp"),
        P("dp", None),
        P("dp", None, None),
        P("dp", None, None),
        P(None, ("dp", "tensor")),
    )
    return jax.shard_map(
        local,
        mesh=mesh,
        in_specs=placed,
        out_specs=(P(("dp", "tensor"), None), P(), P(None, "tensor")),
        check_vma=False,
    )
```

profile of v0, /device:TPU:0, one launch (start us, length us, event | category | flops | bytes accessed | tf_op | source)
XLA Modules:
  0.0 401.9 jit_solution(9235097486257809376)
XLA Ops:
  7.2 0.0 all-gather.7.cloned.1.call-start
  7.2 0.9 convert_element_type.84
  8.1 1.3 fusion.41
  9.4 2.0 fusion.43
  11.4 0.0 all-gather.7.cloned.1.call-update
  11.5 0.0 all-gather.5.cloned.1.call-start
  11.5 0.7 all-gather.5.cloned.1.call-update
  12.2 0.0 reduce-scatter.2.cloned.1.call-start
  12.3 32.6 %all-gather.7.cloned.1.call-done = bf16[512,2048]{1,0:T(8,128)(2,1)} async-done(((bf16[128,2048]{1,0:T(8,128)(2,1)}), bf16[512,2048]{1,0:T(8,128)(2,1)}) %all-gather.7.cloned.1.call-update) | async-done | bytes 2097168 | tf_op jit(solution)/shard_map/all_gather | solution.py:119
  44.9 3.8 fusion.82
  48.7 6.3 %fusion.32 = f32[512,2048]{1,0:T(8,128)} fusion(bf16[352,2048]{1,0:T(8,128)(2,1)S(1)} %copy-done.8, bf16[512,2048]{1,0:T(8,128)(2,1)} %all-gather.7.cloned.1.call-done, bf16[2048,352]{0,1:T(8,128)(2,1)} %param.27, f32[512,352]{0,1:T(8,128)} %fusion.82), kind=kOutput, calls=%fused_computation.29 | convolution fusion | flops 1477476352 | bytes 9895936 | tf_op jit(solution)/shard_map/dot_general | solution.py:19
  55.0 0.0 reduce-scatter.2.cloned.1.call-update
  55.0 0.0 all-gather.11.cloned.1.call-start
  55.1 1.0 copy-done.4
  56.0 1.1 copy.47
  57.2 24.6 %all_gather.15 = bf16[4096,6]{0,1:T(8,128)(2,1)S(1)} all-gather(bf16[128,6]{0,1:T(8,128)(2,1)S(1)} %convert_element_type.79), channel_id=1, replica_groups=mesh['dp'=4,'tensor'=32] {'tensor'}, dimensions={0}, use_global_device_ids=true | all-gather | bytes 50688 | tf_op jit(solution)/shard_map/all_gather | solution.py:84
  81.7 0.1 fusion.63
  81.8 0.3 reduce_window_sum.31
  82.1 38.3 %all-gather.5.cloned.1.call-done = bf16[4096,2048]{1,0:T(8,128)(2,1)} async-done(((bf16[128,2048]{1,0:T(8,128)(2,1)}), bf16[4096,2048]{1,0:T(8,128)(2,1)}) %all-gather.5.cloned.1.call-update) | async-done | bytes 16777232 | tf_op jit(solution)/shard_map/all_gather | solution.py:83
  120.4 8.1 %convolution_convert_fusion = bf16[32,32,2048]{2,1,0:T(8,128)(2,1)S(1)} fusion(bf16[32,128,2048]{2,1,0:T(8,128)(2,1)} %bitcast.109, s32[32,128]{1,0:T(8,128)S(1)} %broadcast_add_fusion.1, pred[32,128]{1,0:T(8,128)(4,1)S(1)} %bitcast.111), kind=kOutput, calls=%fused_computation.16 | convolution fusion | flops 539492352 | bytes 20992000 | tf_op jit(solution)/shard_map/sijc,sid->sjcd/dot_general | solution.py:96
  128.5 2.1 copy-done.1
  130.6 10.7 %fusion.3 = f32[32,32,1408]{2,1,0:T(8,128)} fusion(bf16[32,32,2048]{2,1,0:T(8,128)(2,1)S(1)} %convolution_convert_fusion, bf16[1,2048,1408]{2,1,0:T(8,128)(2,1)} %param.24), kind=kOutput, calls=%fused_computation.4 | convolution fusion | flops 5905580032 | bytes 15728640 | tf_op jit(solution)/shard_map/secd,edf->secf/dot_general | solution.py:102
  141.3 21.0 %convert_bitcast_fusion = bf16[32,1,32,2048]{3,2,1,0:T(8,128)(2,1)} fusion(bf16[1,1408,2048]{2,1,0:T(8,128)(2,1)} %param.25, f32[32,32,1408]{2,1,0:T(8,128)} %fusion.3, bf16[32,32,2048]{2,1,0:T(8,128)(2,1)} %copy-done.1, bf16[1,2048,1408]{2,1,0:T(8,128)(2,1)} %param.23), kind=kOutput, calls=%fused_computation.15 | convolution fusion | flops 11821907968 | bytes 25690112 | tf_op jit(solution)/shard_map/secf,efd->secd/dot_general | solution.py:104
  162.4 5.2 %all-to-all-start = ((bf16[32,1,32,2048]{3,2,1,0:T(8,128)(2,1)}), bf16[32,1,32,2048]{3,2,1,0:T(8,128)(2,1)}, u32[]{:S(2)}, u32[]{:S(2)}) async-start(bf16[32,1,32,2048]{3,2,1,0:T(8,128)(2,1)} %convert_bitcast_fusion), calls=%async_computation | async-start | bytes 8388608 | tf_op jit(solution)/shard_map/all_to_all | solution.py:107
  167.6 0.0 all-gather.9.cloned.1.call-start
  167.7 0.5 all-gather.9.cloned.1.call-update
  168.2 0.3 all-reduce.2.cloned.1.call-start
  168.5 0.1 copy.42
  168.6 0.2 reduce_window_sum.30
  168.8 0.1 copy.43
  168.8 0.1 copy.45
  168.9 0.1 reduce-window.7
  169.0 0.1 reduce.2
  169.1 0.1 convert_reduce_fusion
  169.2 0.1 select_reduce_fusion.1
  169.3 0.1 select_reduce_fusion
  169.5 0.0 reduce-scatter.2.cloned.1.call-done
  169.5 50.9 %all-to-all-done = bf16[32,1,32,2048]{3,2,1,0:T(8,128)(2,1)} async-done(((bf16[32,1,32,2048]{3,2,1,0:T(8,128)(2,1)}), bf16[32,1,32,2048]{3,2,1,0:T(8,128)(2,1)}, u32[]{:S(2)}, u32[]{:S(2)}) %all-to-all-start) | async-done | bytes 4194336 | tf_op jit(solution)/shard_map/all_to_all | solution.py:107
  220.4 4.3 %fusion.23 = f32[128,2048]{1,0:T(8,128)} fusion(f32[128,2048]{1,0:T(8,128)} %reduce-scatter.2.cloned.1.call-done, bf16[32,1,32,2048]{3,2,1,0:T(8,128)(2,1)} %all-to-all-done, s32[128,32]{0,1:T(8,128)S(1)} %copy.43, bf16[128,32]{0,1:T(8,128)(2,1)S(1)} %fusion.68), kind=kOutput, calls=%fused_computation.21 | convolution fusion | flops 537395200 | bytes 6316032 | tf_op jit(solution)/shard_map/kbt,btw->kw/dot_general | solution.py:114
  224.7 9.1 %all-gather.9.cloned.1.call-done = bf16[32,2048,16]{1,2,0:T(8,128)(2,1)} async-done(((bf16[8,2048,16]{1,2,0:T(8,128)(2,1)}), bf16[32,2048,16]{1,2,0:T(8,128)(2,1)}) %all-gather.9.cloned.1.call-update) | async-done | bytes 2097168 | tf_op jit(solution)/shard_map/all_gather | solution.py:128
  233.7 4.5 %fusion.26 = bf16[128,2048]{1,0:T(8,128)(2,1)S(1)} fusion(f32[128,2048]{1,0:T(8,128)} %fusion.23, bf16[32,16,2048]{2,0,1:T(8,128)(2,1)} %all-gather.11.cloned.1.call-done, bf16[32,16,2048]{2,1,0:T(8,128)(2,1)} %bitcast.110, bf16[128,2048]{1,0:T(8,128)(2,1)S(1)} %copy-done.2, pred[128,32]{0,1:T(8,128)(4,1)S(1)} %iota_compare_fusion.3), kind=kOutput, calls=%fused_computation.22 | convolution fusion | flops 537526272 | bytes 6295552 | tf_op jit(solution)/shard_map/dot_general | solution.py:44
  238.3 0.9 fusion.69
  239.2 0.0 all-reduce.2.cloned.1.call-update
  239.2 143.1 %all-reduce.2.cloned.1.call-done = f32[24,2048]{1,0:T(8,128)} async-done(((f32[24,2048]{1,0:T(8,128)}), f32[24,2048]{1,0:T(8,128)}) %all-reduce.2.cloned.1.call-update) | async-done | bytes 196624 | tf_op jit(solution)/shard_map/psum | solution.py:138
  382.3 1.4 convolution_reduce_fusion
  383.7 9.7 %pmax.7 = f32[24,1]{0,1:T(1,128)} all-reduce(f32[24,1]{0,1:T(1,128)S(1)} %bitcast.112), channel_id=1, replica_groups=mesh['dp'=4,'tensor'=32] {'dp'}, use_global_device_ids=true, to_apply=%region_14.15 | all-reduce | flops 24 | bytes 192 | tf_op jit(solution)/shard_map/pmax | solution.py:143
  393.5 1.1 multiply_reduce_fusion
  394.6 0.5 sqrt.3
  (33 shorter events, 0.2 us)
Async XLA Ops:
  7.2 375.2 %copy-start = (bf16[2048,512]{1,0:T(8,128)(2,1)S(1)}, bf16[2048,512]{1,0:T(8,128)(2,1)}, u32[]{:S(2)}) copy-start(bf16[2048,512]{1,0:T(8,128)(2,1)} %param.31) | copy-start | bytes 6291460
  7.2 41.5 %copy-start.8 = (bf16[352,2048]{1,0:T(8,128)(2,1)S(1)}, bf16[352,2048]{1,0:T(8,128)(2,1)}, u32[]{:S(2)}) copy-start(bf16[352,2048]{1,0:T(8,128)(2,1)} %param.28) | copy-start | bytes 4325380
  7.2 37.7 %all-gather.7.cloned.1.call-start = ((), (), s32[]{:S(2)}) async-start(), calls=%async_computation.3 | async-start | bytes 2621440 | tf_op jit(solution)/shard_map/all_gather | solution.py:119
  11.5 109.0 %all-gather.5.cloned.1.call-start = ((), (), s32[]{:S(2)}) async-start(), calls=%async_computation.2 | async-start | bytes 17301504 | tf_op jit(solution)/shard_map/all_gather | solution.py:83
  12.2 157.3 %reduce-scatter.2.cloned.1.call-start = ((), (), s32[]{:S(2)}) async-start(), calls=%async_computation.4 | async-start | bytes 5242880 | tf_op jit(solution)/shard_map/reduce_scatter | solution.py:120
  55.0 1.0 copy-start.4
  55.0 2.1 copy-start.5
  55.0 169.6 %all-gather.11.cloned.1.call-start = ((), (), s32[]{:S(2)}) async-start(), calls=%async_computation.6 | async-start | bytes 2621440 | tf_op jit(solution)/shard_map/all_gather | solution.py:129
  128.5 2.1 copy-start.1
  162.3 6.5 %copy-start.7 = (s32[24]{0:T(128)S(1)}, s32[24]{0:T(128)}, u32[]{:S(2)}) copy-start(s32[24]{0:T(128)} %param.20) | copy-start | bytes 292
  162.3 6.9 %copy-start.9 = (s32[24]{0:T(128)S(1)}, s32[24]{0:T(128)}, u32[]{:S(2)}) copy-start(s32[24]{0:T(128)} %param.21) | copy-start | bytes 292
  162.3 7.0 %copy-start.10 = (s32[32]{0:T(128)S(1)}, s32[32]{0:T(128)}, u32[]{:S(2)}) copy-start(s32[32]{0:T(128)} %param.22) | copy-start | bytes 388
  162.4 7.1 %copy-start.6 = (bf16[128,6]{0,1:T(8,128)(2,1)S(1)}, bf16[128,6]{0,1:T(8,128)(2,1)}, u32[]{:S(2)}) copy-start(bf16[128,6]{0,1:T(8,128)(2,1)} %param.19) | copy-start | bytes 4612
  162.4 58.0 %all-to-all-start = ((bf16[32,1,32,2048]{3,2,1,0:T(8,128)(2,1)}), bf16[32,1,32,2048]{3,2,1,0:T(8,128)(2,1)}, u32[]{:S(2)}, u32[]{:S(2)}) async-start(bf16[32,1,32,2048]{3,2,1,0:T(8,128)(2,1)} %convert_bitcast_fusion), calls=%async_computation | async-start | bytes 8388608 | tf_op jit(solution)/shard_map/all_to_all | solution.py:107
  167.6 66.1 %copy-start.2 = (bf16[128,2048]{1,0:T(8,128)(2,1)S(1)}, bf16[128,2048]{1,0:T(8,128)(2,1)}, u32[]{:S(2)}) copy-start(bf16[128,2048]{1,0:T(8,128)(2,1)} %fusion.43) | copy-start | bytes 1572868
  167.6 66.1 %all-gather.9.cloned.1.call-start = ((), (), s32[]{:S(2)}) async-start(), calls=%async_computation.5 | async-start | bytes 2621440 | tf_op jit(solution)/shard_map/all_gather | solution.py:128
  168.2 214.1 %all-reduce.2.cloned.1.call-start = ((), (), s32[]{:S(2)}) async-start(), calls=%async_computation.7 | async-start | bytes 393216 | tf_op jit(solution)/shard_map/psum | solution.py:138
  238.3 156.8 %copy-start.3 = (bf16[128,2048]{1,0:T(8,128)(2,1)}, bf16[128,2048]{1,0:T(8,128)(2,1)S(1)}, u32[]{:S(2)}) copy-start(bf16[128,2048]{1,0:T(8,128)(2,1)S(1)} %fusion.26) | copy-start | bytes 1572868
Sparse Core Ops, SparseCore 0:
  11.6 33.2 all-gather.6
  47.7 72.6 all-gather.4
  122.8 46.1 reduce-scatter.1
  170.7 30.5 all-gather.10
  202.9 30.8 all-gather.8
  239.3 142.9 all-reduce.1
where the time goes:
time: 402 us
  waiting for transfers between devices  275 us (68%)
  matrix products  61.1 us (15%)
  blocking collectives  34.3 us (9%)
  between operations  14.3 us (4%)
  other arithmetic  6.28 us (2%)
  starting transfers between devices  5.69 us (1%)
  local copies, waits for them, and re-layouts  4.94 us (1%)
    psum x1, waiting for transfers between devices, local(): last_states = lax.psum(last_part, ('dp', 'tensor'))  143 us
    all_to_all x1, waiting for transfers between devices, local(): lax.all_to_all(expert_out, 'tensor', split_axis=0, concat_axis=0, tiled=T...  50.9 us
    all_gather x1, waiting for transfers between devices, local(): lax.all_gather(normed, 'tensor', axis=0, tiled=True)  38.3 us
    all_gather x1, waiting for transfers between devices, local(): peer_rows = lax.all_gather(normed, 'dp', axis=0, tiled=True)  32.6 us
    all_gather x1, blocking collectives, local(): lax.all_gather(routes.astype(jnp.bfloat16), 'tensor', axis=0, tiled=True)  24.6 us
    dot_general x1, matrix products, local(): jnp.einsum('secf,efd->secd', hidden, expert_down, preferred_element_type=...  21 us
    dot_general x1, matrix products, local(): jnp.einsum('secd,edf->secf', incoming, expert_up, preferred_element_type=...  10.7 us
    pmax x1, blocking collectives, local(): block_logit = lax.pmax(jnp.max(logits, axis=1), 'dp')  9.75 us
  transfers between devices with their start and end apart: 7, of which 5 were waited for; matrix products, arithmetic and copies ran while one was open for 14% of the time, Pallas kernels for 0%

commit v1 on v0

--- a/solution.py
+++ b/solution.py
@@ -116,7 +116,9 @@
     )
     own_base = (data_pos * tensor_size + tensor_pos) * tok_rows
     own_positions = own_base + jnp.arange(tok_rows, dtype=jnp.int32)
-    peer_rows = lax.all_gather(normed, "dp", axis=0, tiled=True)
+    peer_rows = jnp.concatenate(
+        lax.all_to_all(jnp.stack(lax.axis_size("dp") * [normed]), "dp", 0, 0), axis=0
+    )
     shared_sum = lax.psum_scatter(
         feed_forward(peer_rows, shared_gate, shared_up_weight, shared_down),
         "dp",

time: 402 us -> 361 us (0.90)
  waiting for transfers between devices: 275 us -> 199 us
  blocking collectives: 34.3 us -> 65.5 us
    all_gather x1, waiting for transfers between devices: 38.3 us -> 4.51 us  [local(): lax.all_gather(normed, 'tensor', axis=0, tiled=True)]
    all_gather x1 -> x0, waiting for transfers between devices: 32.6 us -> none  [local(): peer_rows = lax.all_gather(normed, 'dp', axis=0, tiled=True)]
    all_to_all x0 -> x1, blocking collectives: none -> 30.5 us  [local(): lax.all_to_all(jnp.stack(lax.axis_size('dp') * [normed]), 'dp', 0, 0)]
    all_gather x1, waiting for transfers between devices: 9.08 us -> 0.01 us  [local(): lax.all_gather(adapter_down, 'dp', axis=0, tiled=True)]
  transfers between devices with their start and end apart: 7 -> 6, of which waited for: 5 -> 3; matrix products, arithmetic and copies ran while one was open for 14% -> 16% of each run, Pallas kernels for 0% -> 0%
where the time goes in v1:
time: 361 us; the launch traced here: 360 us
  waiting for transfers between devices  199 us (55%)
  blocking collectives  65.5 us (18%)
  matrix products  60.7 us (17%)
  between operations  15.4 us (4%)
  local copies, waits for them, and re-layouts  7.57 us (2%)
  other arithmetic  6.29 us (2%)
  starting transfers between devices  6.17 us (2%)
    psum x1, waiting for transfers between devices, local(): last_states = lax.psum(last_part, ('dp', 'tensor'))  143 us
    all_to_all x1, waiting for transfers between devices, local(): lax.all_to_all(expert_out, 'tensor', split_axis=0, concat_axis=0, tiled=T...  50.7 us
    all_to_all x1, blocking collectives, local(): lax.all_to_all(jnp.stack(lax.axis_size('dp') * [normed]), 'dp', 0, 0)  30.5 us
    all_gather x1, blocking collectives, local(): lax.all_gather(routes.astype(jnp.bfloat16), 'tensor', axis=0, tiled=True)  25.2 us
    dot_general x1, matrix products, local(): jnp.einsum('secf,efd->secd', hidden, expert_down, preferred_element_type=...  21.1 us
    dot_general x1, matrix products, local(): jnp.einsum('secd,edf->secf', incoming, expert_up, preferred_element_type=...  10.4 us
    pmax x1, blocking collectives, local(): block_logit = lax.pmax(jnp.max(logits, axis=1), 'dp')  9.8 us
    dot_general x1, matrix products, local(): jnp.einsum('sijc,sid->sjcd', source_pick, pooled, preferred_element_type=...  8.18 us
  transfers between devices with their start and end apart: 6, of which 3 were waited for; matrix products, arithmetic and copies ran while one was open for 16% of the time, Pallas kernels for 0%

profile of v1, /device:TPU:0, one launch (start us, length us, event | category | flops | bytes accessed | tf_op | source)
XLA Modules:
  0.0 360.4 jit_solution(13782004751530897071)
XLA Ops:
  8.0 0.0 all-gather.4.cloned.1.call-start
  8.1 0.8 convert_element_type.84
  8.9 1.2 fusion.41
  10.1 2.1 fusion.43
  12.3 0.0 all-gather.4.cloned.1.call-update
  12.3 0.0 reduce-scatter.2.cloned.1.call-start
  12.3 1.3 stack.2
  13.6 30.5 %all_to_all.10 = bf16[4,128,2048]{2,1,0:T(8,128)(2,1)S(1)} all-to-all(bf16[4,128,2048]{2,1,0:T(8,128)(2,1)S(1)} %stack.2), channel_id=1, replica_groups=mesh['dp'=4,'tensor'=32] {'dp'}, dimensions={0} | all-to-all | bytes 4194304 | tf_op jit(solution)/shard_map/all_to_all | solution.py:120
  44.1 1.3 copy-done.3
  45.5 1.8 fusion.82
  47.3 8.1 %fusion.32 = f32[512,2048]{1,0:T(8,128)} fusion(bf16[352,2048]{1,0:T(8,128)(2,1)} %param.28, bf16[512,2048]{1,0:T(8,128)(2,1)} %bitcast.112, bf16[2048,352]{0,1:T(8,128)(2,1)} %param.27, f32[512,352]{0,1:T(8,128)} %fusion.82), kind=kOutput, calls=%fused_computation.29 | convolution fusion | flops 1477476352 | bytes 9895936 | tf_op jit(solution)/shard_map/dot_general | solution.py:19
  55.4 0.0 reduce-scatter.2.cloned.1.call-update
  55.5 0.0 all-gather.8.cloned.1.call-start
  55.5 1.0 copy-done.5
  56.5 1.1 copy.47
  57.6 0.0 all-gather.8.cloned.1.call-update
  57.6 25.2 %all_gather.12 = bf16[4096,6]{0,1:T(8,128)(2,1)S(1)} all-gather(bf16[128,6]{0,1:T(8,128)(2,1)S(1)} %convert_element_type.79), channel_id=1, replica_groups=mesh['dp'=4,'tensor'=32] {'tensor'}, dimensions={0}, use_global_device_ids=true | all-gather | bytes 50688 | tf_op jit(solution)/shard_map/all_gather | solution.py:84
  82.8 0.1 fusion.63
  82.9 0.3 reduce_window_sum.31
  83.2 4.5 %all-gather.4.cloned.1.call-done = bf16[4096,2048]{1,0:T(8,128)(2,1)} async-done(((bf16[128,2048]{1,0:T(8,128)(2,1)}), bf16[4096,2048]{1,0:T(8,128)(2,1)}) %all-gather.4.cloned.1.call-update) | async-done | bytes 16777232 | tf_op jit(solution)/shard_map/all_gather | solution.py:83
  87.7 8.2 %convolution_convert_fusion = bf16[32,32,2048]{2,1,0:T(8,128)(2,1)S(1)} fusion(bf16[32,128,2048]{2,1,0:T(8,128)(2,1)} %bitcast.110, s32[32,128]{1,0:T(8,128)S(1)} %broadcast_add_fusion.1, pred[32,128]{1,0:T(8,128)(4,1)S(1)} %bitcast.114), kind=kOutput, calls=%fused_computation.16 | convolution fusion | flops 539492352 | bytes 20992000 | tf_op jit(solution)/shard_map/sijc,sid->sjcd/dot_general | solution.py:96
  95.9 2.1 copy-done.1
  98.0 10.4 %fusion.3 = f32[32,32,1408]{2,1,0:T(8,128)} fusion(bf16[32,32,2048]{2,1,0:T(8,128)(2,1)S(1)} %convolution_convert_fusion, bf16[1,2048,1408]{2,1,0:T(8,128)(2,1)} %param.24), kind=kOutput, calls=%fused_computation.4 | convolution fusion | flops 5905580032 | bytes 15728640 | tf_op jit(solution)/shard_map/secd,edf->secf/dot_general | solution.py:102
  108.3 21.1 %convert_bitcast_fusion = bf16[32,1,32,2048]{3,2,1,0:T(8,128)(2,1)} fusion(bf16[1,1408,2048]{2,1,0:T(8,128)(2,1)} %param.25, f32[32,32,1408]{2,1,0:T(8,128)} %fusion.3, bf16[32,32,2048]{2,1,0:T(8,128)(2,1)} %copy-done.1, bf16[1,2048,1408]{2,1,0:T(8,128)(2,1)} %param.23), kind=kOutput, calls=%fused_computation.15 | convolution fusion | flops 11821907968 | bytes 25690112 | tf_op jit(solution)/shard_map/secf,efd->secd/dot_general | solution.py:104
  129.4 5.7 %all-to-all-start = ((bf16[32,1,32,2048]{3,2,1,0:T(8,128)(2,1)}), bf16[32,1,32,2048]{3,2,1,0:T(8,128)(2,1)}, u32[]{:S(2)}, u32[]{:S(2)}) async-start(bf16[32,1,32,2048]{3,2,1,0:T(8,128)(2,1)} %convert_bitcast_fusion), calls=%async_computation | async-start | bytes 8388608 | tf_op jit(solution)/shard_map/all_to_all | solution.py:107
  135.2 0.0 all-gather.6.cloned.1.call-start
  135.2 0.7 all-gather.6.cloned.1.call-update
  135.9 0.3 all-reduce.2.cloned.1.call-start
  136.2 0.1 copy.42
  136.3 0.2 reduce_window_sum.30
  136.5 0.1 copy.43
  136.6 0.1 copy.45
  136.7 0.1 reduce-window.7
  136.7 0.1 reduce.2
  136.8 0.1 convert_reduce_fusion
  136.9 0.1 select_reduce_fusion.1
  137.0 0.1 select_reduce_fusion
  137.2 0.0 reduce-scatter.2.cloned.1.call-done
  137.2 50.7 %all-to-all-done = bf16[32,1,32,2048]{3,2,1,0:T(8,128)(2,1)} async-done(((bf16[32,1,32,2048]{3,2,1,0:T(8,128)(2,1)}), bf16[32,1,32,2048]{3,2,1,0:T(8,128)(2,1)}, u32[]{:S(2)}, u32[]{:S(2)}) %all-to-all-start) | async-done | bytes 4194336 | tf_op jit(solution)/shard_map/all_to_all | solution.py:107
  187.9 4.2 %fusion.23 = f32[128,2048]{1,0:T(8,128)} fusion(f32[128,2048]{1,0:T(8,128)} %reduce-scatter.2.cloned.1.call-done, bf16[32,1,32,2048]{3,2,1,0:T(8,128)(2,1)} %all-to-all-done, s32[128,32]{0,1:T(8,128)S(1)} %copy.43, bf16[128,32]{0,1:T(8,128)(2,1)S(1)} %fusion.68), kind=kOutput, calls=%fused_computation.21 | convolution fusion | flops 537395200 | bytes 6316032 | tf_op jit(solution)/shard_map/kbt,btw->kw/dot_general | solution.py:114
  192.2 4.5 %fusion.26 = bf16[128,2048]{1,0:T(8,128)(2,1)S(1)} fusion(f32[128,2048]{1,0:T(8,128)} %fusion.23, bf16[32,16,2048]{2,0,1:T(8,128)(2,1)} %all-gather.8.cloned.1.call-done, bf16[32,16,2048]{2,1,0:T(8,128)(2,1)} %bitcast.113, bf16[128,2048]{1,0:T(8,128)(2,1)S(1)} %copy-done.2, pred[128,32]{0,1:T(8,128)(4,1)S(1)} %iota_compare_fusion.3), kind=kOutput, calls=%fused_computation.22 | convolution fusion | flops 537526272 | bytes 6295552 | tf_op jit(solution)/shard_map/dot_general | solution.py:44
  196.7 0.9 fusion.69
  197.6 0.0 all-reduce.2.cloned.1.call-update
  197.6 142.8 %all-reduce.2.cloned.1.call-done = f32[24,2048]{1,0:T(8,128)} async-done(((f32[24,2048]{1,0:T(8,128)}), f32[24,2048]{1,0:T(8,128)}) %all-reduce.2.cloned.1.call-update) | async-done | bytes 196624 | tf_op jit(solution)/shard_map/psum | solution.py:140
  340.5 1.4 convolution_reduce_fusion
  341.9 9.8 %pmax.7 = f32[24,1]{0,1:T(1,128)} all-reduce(f32[24,1]{0,1:T(1,128)S(1)} %bitcast.115), channel_id=1, replica_groups=mesh['dp'=4,'tensor'=32] {'dp'}, use_global_device_ids=true, to_apply=%region_14.15 | all-reduce | flops 24 | bytes 192 | tf_op jit(solution)/shard_map/pmax | solution.py:145
  351.7 1.1 multiply_reduce_fusion
  352.7 0.5 sqrt.3
  (34 shorter events, 0.1 us)
Async XLA Ops:
  8.0 332.5 %copy-start = (bf16[2048,512]{1,0:T(8,128)(2,1)S(1)}, bf16[2048,512]{1,0:T(8,128)(2,1)}, u32[]{:S(2)}) copy-start(bf16[2048,512]{1,0:T(8,128)(2,1)} %param.31) | copy-start | bytes 6291460
  8.0 79.7 %all-gather.4.cloned.1.call-start = ((), (), s32[]{:S(2)}) async-start(), calls=%async_computation.3 | async-start | bytes 17301504 | tf_op jit(solution)/shard_map/all_gather | solution.py:83
  10.1 35.3 %copy-start.9 = (bf16[2048,352]{0,1:T(8,128)(2,1)S(1)}, bf16[2048,352]{0,1:T(8,128)(2,1)}, u32[]{:S(2)}) copy-start(bf16[2048,352]{0,1:T(8,128)(2,1)} %param.26) | copy-start | bytes 4325380
  12.3 124.9 %reduce-scatter.2.cloned.1.call-start = ((), (), s32[]{:S(2)}) async-start(), calls=%async_computation.4 | async-start | bytes 5242880 | tf_op jit(solution)/shard_map/reduce_scatter | solution.py:122
  44.1 1.3 copy-start.3
  55.4 1.1 copy-start.5
  55.4 2.2 copy-start.6
  55.5 136.7 %all-gather.8.cloned.1.call-start = ((), (), s32[]{:S(2)}) async-start(), calls=%async_computation.6 | async-start | bytes 2621440 | tf_op jit(solution)/shard_map/all_gather | solution.py:131
  95.9 2.1 copy-start.1
  129.4 7.2 %copy-start.8 = (s32[24]{0:T(128)S(1)}, s32[24]{0:T(128)}, u32[]{:S(2)}) copy-start(s32[24]{0:T(128)} %param.20) | copy-start | bytes 292
  129.4 7.5 %copy-start.10 = (s32[24]{0:T(128)S(1)}, s32[24]{0:T(128)}, u32[]{:S(2)}) copy-start(s32[24]{0:T(128)} %param.21) | copy-start | bytes 292
  129.4 7.6 %copy-start.11 = (s32[32]{0:T(128)S(1)}, s32[32]{0:T(128)}, u32[]{:S(2)}) copy-start(s32[32]{0:T(128)} %param.22) | copy-start | bytes 388
  129.4 7.7 %copy-start.7 = (bf16[128,6]{0,1:T(8,128)(2,1)S(1)}, bf16[128,6]{0,1:T(8,128)(2,1)}, u32[]{:S(2)}) copy-start(bf16[128,6]{0,1:T(8,128)(2,1)} %param.19) | copy-start | bytes 4612
  129.4 58.5 %all-to-all-start = ((bf16[32,1,32,2048]{3,2,1,0:T(8,128)(2,1)}), bf16[32,1,32,2048]{3,2,1,0:T(8,128)(2,1)}, u32[]{:S(2)}, u32[]{:S(2)}) async-start(bf16[32,1,32,2048]{3,2,1,0:T(8,128)(2,1)} %convert_bitcast_fusion), calls=%async_computation | async-start | bytes 8388608 | tf_op jit(solution)/shard_map/all_to_all | solution.py:107
  135.2 57.0 %copy-start.2 = (bf16[128,2048]{1,0:T(8,128)(2,1)S(1)}, bf16[128,2048]{1,0:T(8,128)(2,1)}, u32[]{:S(2)}) copy-start(bf16[128,2048]{1,0:T(8,128)(2,1)} %fusion.43) | copy-start | bytes 1572868
  135.2 57.0 %all-gather.6.cloned.1.call-start = ((), (), s32[]{:S(2)}) async-start(), calls=%async_computation.5 | async-start | bytes 2621440 | tf_op jit(solution)/shard_map/all_gather | solution.py:130
  135.9 204.5 %all-reduce.2.cloned.1.call-start = ((), (), s32[]{:S(2)}) async-start(), calls=%async_computation.7 | async-start | bytes 393216 | tf_op jit(solution)/shard_map/psum | solution.py:140
  196.7 156.6 %copy-start.4 = (bf16[128,2048]{1,0:T(8,128)(2,1)}, bf16[128,2048]{1,0:T(8,128)(2,1)S(1)}, u32[]{:S(2)}) copy-start(bf16[128,2048]{1,0:T(8,128)(2,1)S(1)} %fusion.26) | copy-start | bytes 1572868
Sparse Core Ops, SparseCore 0:
  12.4 75.2 all-gather.3
  89.4 30.1 all-gather.7
  137.8 31.9 all-gather.5
Sparse Core Ops, SparseCore 1:
  55.5 47.0 reduce-scatter.1
  197.7 142.7 all-reduce.1
